TPU v7x, 256 devices: a whole 4x4x8 slice. The times are simulated.
256 devices in a mesh: outer: 32 (over z_lo, x, core), inner: 8 (over y, z_hi).
Axes of the slice: x: 4, y: 4, z: 8 (z_hi: 2, z_lo: 4; z = z_hi * 4 + z_lo), core: 2. Of those that a mesh axis runs over, the one named last changes fastest.
Arguments:
- qkv: bfloat16 [16384, 8, 10, 128], P(('outer', 'inner')), may hold values from -96 to 96
- key_codes: int32 [4096, 8, 16], P('outer', 'inner'), may hold values from 0 to 255
- codebooks: bfloat16 [8, 256, 128], P('inner'), may hold values from -4 to 4
- value_codes: bfloat16 [4096, 8, 128], P('outer', 'inner'), may hold values from -4 to 4
- value_scales: float32 [4096, 8], P('outer', 'inner'), may hold values from 0.25 to 4
- block_ids: int32 [32], P('outer'), may hold values from 0 to 31, each once
Outputs:
- attended: bfloat16 [16384, 8, 8, 128], P(('outer', 'inner'))
All inputs are finite; a program needn't handle non-finite values.
Results may differ from a plain program's by a relative error of at most 0.011.
Values may be sent and summed in bfloat16 or wider, within the bound.
A program may use at most 64 MiB of HBM per device.

v0:
```python
import math
import jax
import jax.numpy as jnp
from jax import lax
from jax.sharding import PartitionSpec as P

rope_base = 500000.0


def rotate(tensor, position):
    half_dim = tensor.shape[-1] // 2
    ladder = jnp.arange(half_dim, dtype=jnp.float32)
    inverse = jnp.exp(ladder * jnp.float32(-2.0 * math.log(rope_base) / tensor.shape[-1]))
    angles = position.astype(jnp.float32)[:, None] * inverse[None, :]
    target = (position.shape[0],) + (1,) * (tensor.ndim - 2) + (half_dim,)
    cosine = jnp.cos(angles).reshape(target)
    sine_part = jnp.sin(angles).reshape(target)
    floats = tensor.astype(jnp.float32)
    first_half = floats[..., :half_dim]
    second_half = floats[..., half_dim:]
    return jnp.concatenate(
        [
            first_half * cosine - second_half * sine_part,
            second_half * cosine + first_half * sine_part,
        ],
        axis=-1,
    )


def decode_block(key_codes, codebooks):
    block_rows, kv_local, group_count = key_codes.shape
    entries = codebooks.shape[1]
    head_dim = codebooks.shape[2]
    ladder = lax.broadcasted_iota(jnp.int32, (1, 1, 1, entries), 3).astype(jnp.float32)
    one_hot = (key_codes.astype(jnp.float32)[..., None] == ladder).astype(jnp.bfloat16)
    code_table = codebooks.reshape(kv_local, entries, group_count, head_dim // group_count)
    decoded = jnp.einsum("bkgc,kcgd->bkgd", one_hot, code_table, preferred_element_type=jnp.float32)
    return decoded.reshape(block_rows, kv_local, head_dim)


def span_of():
    return 1024


def absorb(state, queries, key_rows, value_rows, allowed):
    running_max, running_sum, weighted = state
    scores = jnp.einsum(
        "tkgd,nkd->tkgn", queries, key_rows, preferred_element_type=jnp.float32
    ) * queries.shape[-1] ** (-0.5)
    if allowed is not None:
        scores = jnp.where(allowed[:, None, None, :], scores, -jnp.inf)
    new_max = jnp.maximum(running_max, jnp.max(scores, axis=-1))
    decay_factor = jnp.exp(running_max - new_max)
    weights = jnp.exp(scores - new_max[..., None])
    running_sum = running_sum * decay_factor + jnp.sum(weights, axis=-1)
    weighted = weighted * decay_factor[..., None] + jnp.einsum(
        "tkgn,nkd->tkgd",
        weights.astype(jnp.bfloat16),
        value_rows,
        preferred_element_type=jnp.float32,
    )
    return (new_max, running_sum, weighted)


def shards(qkv, key_codes, codebooks, value_codes, value_scales, block_ids):
    group_heads = qkv.shape[2] - 2
    head_dim = qkv.shape[3]
    block_rows = key_codes.shape[0]
    prefix_len = block_rows * lax.axis_size("outer")
    prefix_values = (value_codes.astype(jnp.float32) * value_scales[:, :, None]).astype(
        jnp.bfloat16
    )
    exchanged = lax.all_to_all(qkv, "inner", split_axis=1, concat_axis=0, tiled=True)
    stretch_rows = exchanged.shape[0]
    kv_local = exchanged.shape[1]
    local_pos = jnp.arange(stretch_rows, dtype=jnp.int32)
    stretch_pos = prefix_len + local_pos
    queries = rotate(exchanged[:, :, :group_heads, :], stretch_pos).astype(jnp.bfloat16)
    stretch_keys = rotate(exchanged[:, :, group_heads, :], stretch_pos).astype(jnp.bfloat16)
    stretch_values = exchanged[:, :, group_heads + 1, :]
    initial = (
        jnp.full((stretch_rows, kv_local, group_heads), -1e30, jnp.float32),
        jnp.zeros((stretch_rows, kv_local, group_heads), jnp.float32),
        jnp.zeros((stretch_rows, kv_local, group_heads, head_dim), jnp.float32),
    )
    own_pos = block_ids[0] * block_rows + jnp.arange(block_rows, dtype=jnp.int32)
    prefix_keys = rotate(decode_block(key_codes, codebooks), own_pos).astype(jnp.bfloat16)
    key_rows = lax.all_gather(prefix_keys, "outer", axis=0, tiled=True)
    value_rows = lax.all_gather(prefix_values, "outer", axis=0, tiled=True)
    length = key_rows.shape[0]
    span_rows = span_of()

    def advance(step_index, inner_state):
        first_row = step_index * span_rows
        key_part = lax.dynamic_slice_in_dim(key_rows, first_row, span_rows, 0)
        value_part = lax.dynamic_slice_in_dim(value_rows, first_row, span_rows, 0)
        return absorb(inner_state, queries, key_part, value_part, None)

    allowed = local_pos[None, :] <= local_pos[:, None]
    final_state = absorb(
        lax.fori_loop(0, length // span_rows, advance, initial),
        queries,
        stretch_keys,
        stretch_values,
        allowed,
    )
    running_max, running_sum, weighted = final_state
    outputs = (weighted / running_sum[..., None]).astype(jnp.bfloat16)
    return lax.all_to_all(outputs, "inner", split_axis=0, concat_axis=1, tiled=True)


def solution(mesh):
    return jax.shard_map(
        shards,
        mesh=mesh,
        in_specs=(
            P(("outer", "inner"), None, None, None),
            P("outer", "inner", None),
            P("inner", None, None),
            P("outer", "inner", None),
            P("outer", "inner"),
            P("outer"),
        ),
        out_specs=P(("outer", "inner"), None, None, None),
        check_vma=False,
    )
```

profile of v0, /device:TPU:32, one launch (start us, length us, event | category | flops | bytes accessed | tf_op | source)
XLA Modules:
  0.0 320.7 jit_solution(219991064677124452)
XLA Ops:
  11.8 10.2 %all-to-all-start = ((bf16[64,8,10,128]{3,0,2,1:T(8,128)(2,1)}), bf16[64,8,10,128]{3,0,2,1:T(8,128)(2,1)S(1)}, u32[]{:S(2)}, u32[]{:S(2)}) async-start(bf16[64,8,10,128]{3,0,2,1:T(8,128)(2,1)} %copy.49), calls=%async_computation | async-start | bytes 2621440 | tf_op jit(solution)/shard_map/all_to_all | solution.py:73
  23.6 1.8 multiply_cosine_fusion.1
  25.4 35.3 %all-to-all-done = bf16[64,8,10,128]{3,0,2,1:T(8,128)(2,1)S(1)} async-done(((bf16[64,8,10,128]{3,0,2,1:T(8,128)(2,1)}), bf16[64,8,10,128]{3,0,2,1:T(8,128)(2,1)S(1)}, u32[]{:S(2)}, u32[]{:S(2)}) %all-to-all-start) | async-done | bytes 1310752 | tf_op jit(solution)/shard_map/all_to_all | solution.py:73
  65.3 25.1 %all-gather.3.cloned.1.call-done = bf16[4096,1,128]{0,2,1:T(8,128)(2,1)} async-done(((bf16[128,1,128]{0,2,1:T(8,128)(2,1)}), bf16[4096,1,128]{0,2,1:T(8,128)(2,1)}) %all-gather.3.cloned.1.call-update) | async-done | bytes 1048592 | tf_op jit(solution)/shard_map/all_gather | solution.py:88
  90.4 67.9 %all-gather.5.cloned.1.call-done = bf16[4096,1,128]{0,2,1:T(8,128)(2,1)} async-done(((bf16[128,1,128]{0,2,1:T(8,128)(2,1)}), bf16[4096,1,128]{0,2,1:T(8,128)(2,1)}) %all-gather.5.cloned.1.call-update) | async-done | bytes 1048592 | tf_op jit(solution)/shard_map/all_gather | solution.py:89
  158.4 101.3 %while.18 = (s32[]{:T(128)}, f32[512,1,8]{0,2,1:T(8,128)S(1)}, f32[512,1,8]{0,2,1:T(8,128)S(1)}, f32[512,1,8,128]{0,3,2,1:T(8,128)S(1)}, bf16[4096,1,128]{0,2,1:...) while((s32[]{:T(128)}, f32[512,1,8]{0,2,1:T(8,128)S(1)}, ...), condition=%wide.region_3.0_spmd.clone, body=%wide.region_0.0_spmd.clone.sunk | while | flops 2182635520 | bytes 56361140 | solution.py:101
  158.4 9.1 %bitcast_reduce_fusion.2 = (f32[512,8]{0,1:T(8,128)S(1)}, f32[1024,512,8]{1,0,2:T(8,128)}) fusion(bf16[512,1,8,128]{3,0,2,1:T(8,128)(2,1)S(1)} %get-tuple-element.273, bf16[4096,1,128]{0,2,1:T(8,128)(2,1)} %get-tuple-element.272, s32[]{:T(128)S(6)} %select_n.27), kind=kOutput, calls=%fused_computation.1.clone.1 | convolution fusion | flops 1082126336 | bytes 18104324 | tf_op jit(solution)/shard_map/while/body/eval_jaxpr/tkgd,nkd->tkgn/dot_general | solution.py:47
  167.5 8.5 %fusion.77 = f32[512,8]{0,1:T(8,128)S(1)} fusion(f32[1024,512,8]{1,0,2:T(8,128)} %get-tuple-element.244, f32[512,8]{0,1:T(8,128)S(1)} %bitcast.167), kind=kLoop, calls=%fused_computation.4.clone.1 | loop fusion | flops 12578816 | bytes 16809984 | tf_op jit(solution)/shard_map/while/body/eval_jaxpr/reduce_sum | solution.py:55
  176.0 7.7 %bitcast_add_fusion.7 = f32[512,1,8,128]{0,3,2,1:T(8,128)S(1)} fusion(f32[512,1,8,128]{0,3,2,1:T(8,128)S(1)} %get-tuple-element.260, f32[1024,512,8]{1,0,2:T(8,128)} %get-tuple-element.244, f32[512,8]{0,1:T(8,128)S(1)} %bitcast.168, f32[512,8]{0,1:T(8,128)S(1)} %get-tuple-element.245, pred[]{:T(512)S(6)} %compare.3, ...), kind=kOutput, calls=%fused_computation.9.clone.1 | convolution fusion | flops 1087897600 | bytes 21266436 | tf_op jit(solution)/shard_map/while/body/eval_jaxpr/tkgn,nkd->tkgd/dot_general | solution.py:56
  183.7 9.1 %bitcast_reduce_fusion.2 = (f32[512,8]{0,1:T(8,128)S(1)}, f32[1024,512,8]{1,0,2:T(8,128)}) fusion(bf16[512,1,8,128]{3,0,2,1:T(8,128)(2,1)S(1)} %get-tuple-element.273, bf16[4096,1,128]{0,2,1:T(8,128)(2,1)} %get-tuple-element.272, s32[]{:T(128)S(6)} %select_n.27), kind=kOutput, calls=%fused_computation.1.clone.1 | convolution fusion | flops 1082126336 | bytes 18104324 | tf_op jit(solution)/shard_map/while/body/eval_jaxpr/tkgd,nkd->tkgn/dot_general | solution.py:47
  192.8 8.5 %fusion.77 = f32[512,8]{0,1:T(8,128)S(1)} fusion(f32[1024,512,8]{1,0,2:T(8,128)} %get-tuple-element.244, f32[512,8]{0,1:T(8,128)S(1)} %bitcast.167), kind=kLoop, calls=%fused_computation.4.clone.1 | loop fusion | flops 12578816 | bytes 16809984 | tf_op jit(solution)/shard_map/while/body/eval_jaxpr/reduce_sum | solution.py:55
  201.3 7.7 %bitcast_add_fusion.7 = f32[512,1,8,128]{0,3,2,1:T(8,128)S(1)} fusion(f32[512,1,8,128]{0,3,2,1:T(8,128)S(1)} %get-tuple-element.260, f32[1024,512,8]{1,0,2:T(8,128)} %get-tuple-element.244, f32[512,8]{0,1:T(8,128)S(1)} %bitcast.168, f32[512,8]{0,1:T(8,128)S(1)} %get-tuple-element.245, pred[]{:T(512)S(6)} %compare.3, ...), kind=kOutput, calls=%fused_computation.9.clone.1 | convolution fusion | flops 1087897600 | bytes 21266436 | tf_op jit(solution)/shard_map/while/body/eval_jaxpr/tkgn,nkd->tkgd/dot_general | solution.py:56
  209.0 9.1 %bitcast_reduce_fusion.2 = (f32[512,8]{0,1:T(8,128)S(1)}, f32[1024,512,8]{1,0,2:T(8,128)}) fusion(bf16[512,1,8,128]{3,0,2,1:T(8,128)(2,1)S(1)} %get-tuple-element.273, bf16[4096,1,128]{0,2,1:T(8,128)(2,1)} %get-tuple-element.272, s32[]{:T(128)S(6)} %select_n.27), kind=kOutput, calls=%fused_computation.1.clone.1 | convolution fusion | flops 1082126336 | bytes 18104324 | tf_op jit(solution)/shard_map/while/body/eval_jaxpr/tkgd,nkd->tkgn/dot_general | solution.py:47
  218.1 8.5 %fusion.77 = f32[512,8]{0,1:T(8,128)S(1)} fusion(f32[1024,512,8]{1,0,2:T(8,128)} %get-tuple-element.244, f32[512,8]{0,1:T(8,128)S(1)} %bitcast.167), kind=kLoop, calls=%fused_computation.4.clone.1 | loop fusion | flops 12578816 | bytes 16809984 | tf_op jit(solution)/shard_map/while/body/eval_jaxpr/reduce_sum | solution.py:55
  226.7 7.7 %bitcast_add_fusion.7 = f32[512,1,8,128]{0,3,2,1:T(8,128)S(1)} fusion(f32[512,1,8,128]{0,3,2,1:T(8,128)S(1)} %get-tuple-element.260, f32[1024,512,8]{1,0,2:T(8,128)} %get-tuple-element.244, f32[512,8]{0,1:T(8,128)S(1)} %bitcast.168, f32[512,8]{0,1:T(8,128)S(1)} %get-tuple-element.245, pred[]{:T(512)S(6)} %compare.3, ...), kind=kOutput, calls=%fused_computation.9.clone.1 | convolution fusion | flops 1087897600 | bytes 21266436 | tf_op jit(solution)/shard_map/while/body/eval_jaxpr/tkgn,nkd->tkgd/dot_general | solution.py:56
  234.4 9.1 %bitcast_reduce_fusion.2 = (f32[512,8]{0,1:T(8,128)S(1)}, f32[1024,512,8]{1,0,2:T(8,128)}) fusion(bf16[512,1,8,128]{3,0,2,1:T(8,128)(2,1)S(1)} %get-tuple-element.273, bf16[4096,1,128]{0,2,1:T(8,128)(2,1)} %get-tuple-element.272, s32[]{:T(128)S(6)} %select_n.27), kind=kOutput, calls=%fused_computation.1.clone.1 | convolution fusion | flops 1082126336 | bytes 18104324 | tf_op jit(solution)/shard_map/while/body/eval_jaxpr/tkgd,nkd->tkgn/dot_general | solution.py:47
  243.5 8.5 %fusion.77 = f32[512,8]{0,1:T(8,128)S(1)} fusion(f32[1024,512,8]{1,0,2:T(8,128)} %get-tuple-element.244, f32[512,8]{0,1:T(8,128)S(1)} %bitcast.167), kind=kLoop, calls=%fused_computation.4.clone.1 | loop fusion | flops 12578816 | bytes 16809984 | tf_op jit(solution)/shard_map/while/body/eval_jaxpr/reduce_sum | solution.py:55
  252.0 7.7 %bitcast_add_fusion.7 = f32[512,1,8,128]{0,3,2,1:T(8,128)S(1)} fusion(f32[512,1,8,128]{0,3,2,1:T(8,128)S(1)} %get-tuple-element.260, f32[1024,512,8]{1,0,2:T(8,128)} %get-tuple-element.244, f32[512,8]{0,1:T(8,128)S(1)} %bitcast.168, f32[512,8]{0,1:T(8,128)S(1)} %get-tuple-element.245, pred[]{:T(512)S(6)} %compare.3, ...), kind=kOutput, calls=%fused_computation.9.clone.1 | convolution fusion | flops 1087897600 | bytes 21266436 | tf_op jit(solution)/shard_map/while/body/eval_jaxpr/tkgn,nkd->tkgd/dot_general | solution.py:56
  259.7 1.8 copy.53
  261.5 2.4 fusion.54
  263.9 3.4 %fusion.22 = (f32[512,8]{0,1:T(8,128)S(1)}, f32[512,512,8]{1,0,2:T(8,128)S(1)}) fusion(pred[512,512]{0,1:T(8,128)(4,1)S(1)} %copy-done.4, bf16[512,8,64]{2,0,1:T(8,128)(2,1)} %bitcast.170, bf16[512,8,64]{2,0,1:T(8,128)(2,1)S(1)} %bitcast.169, bf16[512,64]{1,0:T(8,128)(2,1)S(1)} %get-tuple-element.186, bf16[512,64]{1,0:T(8,128)(2,1)S(1)} %get-tuple-element.185), kind=kOutput, calls=%fused_computation.29 | convolution fusion | flops 545517568 | bytes 9846784 | tf_op jit(solution)/shard_map/tkgd,nkd->tkgn/dot_general | solution.py:47
  267.4 1.7 fusion.20
  269.2 4.1 %fusion.28 = bf16[512,1,8,128]{3,0,2,1:T(8,128)(2,1)S(1)} fusion(f32[512,1,8,128]{3,0,2,1:T(8,128)S(1)} %copy-done.5, f32[512,512,8]{1,0,2:T(8,128)S(1)} %get-tuple-element.194, f32[512,8]{0,1:T(8,128)S(1)} %fusion.65, pred[512,512]{0,1:T(8,128)(4,1)S(1)} %copy-done.4, f32[512,8]{0,1:T(8,128)S(1)} %get-tuple-element.190, ...), kind=kOutput, calls=%fused_computation.35 | convolution fusion | flops 547356672 | bytes 11976704 | tf_op jit(solution)/shard_map/tkgn,nkd->tkgd/dot_general | solution.py:56
  274.0 38.6 %all_to_all.36 = bf16[512,1,8,128]{3,2,1,0:T(8,128)(2,1)S(1)} all-to-all(bf16[512,1,8,128]{3,2,1,0:T(8,128)(2,1)S(1)} %copy.55), channel_id=1, replica_groups=mesh['outer'=32,'inner'=8] {'inner'}, dimensions={0} | all-to-all | bytes 2097152 | tf_op jit(solution)/shard_map/all_to_all | solution.py:109
  (63 shorter events, 12.7 us)
Async XLA Ops:
  6.5 3.8 %copy-start.6 = (bf16[64,8,10,128]{3,1,2,0:T(8,128)(2,1)S(1)}, bf16[64,8,10,128]{3,1,2,0:T(8,128)(2,1)}, u32[]{:S(2)}) copy-start(bf16[64,8,10,128]{3,1,2,0:T(8,128)(2,1)} %param.8) | copy-start | bytes 3932164
  6.5 83.9 %all-gather.3.cloned.1.call-start = ((), (), s32[]{:S(2)}) async-start(), calls=%async_computation.2 | async-start | bytes 1081344 | tf_op jit(solution)/shard_map/all_gather | solution.py:88
  10.3 11.7 %copy-start.9 = (bf16[128,1,128]{2,0,1:T(8,128)(2,1)S(1)}, bf16[128,1,128]{2,0,1:T(8,128)(2,1)}, u32[]{:S(2)}) copy-start(bf16[128,1,128]{2,0,1:T(8,128)(2,1)} %param.11) | copy-start | bytes 98308
  10.3 11.8 %copy-start.10 = (f32[128,1]{0,1:T(1,128)S(1)}, f32[128,1]{0,1:T(1,128)}, u32[]{:S(2)}) copy-start(f32[128,1]{0,1:T(1,128)} %param.12) | copy-start | bytes 1540
  11.8 48.9 %all-to-all-start = ((bf16[64,8,10,128]{3,0,2,1:T(8,128)(2,1)}), bf16[64,8,10,128]{3,0,2,1:T(8,128)(2,1)S(1)}, u32[]{:S(2)}, u32[]{:S(2)}) async-start(bf16[64,8,10,128]{3,0,2,1:T(8,128)(2,1)} %copy.49), calls=%async_computation | async-start | bytes 2621440 | tf_op jit(solution)/shard_map/all_to_all | solution.py:73
  22.0 136.4 %all-gather.5.cloned.1.call-start = ((), (), s32[]{:S(2)}) async-start(), calls=%async_computation.3 | async-start | bytes 1081344 | tf_op jit(solution)/shard_map/all_gather | solution.py:89
  60.8 3.7 %copy-start.3 = (bf16[8,64,1,10,128]{4,1,0,3,2:T(8,128)(2,1)}, bf16[8,64,1,10,128]{4,1,0,3,2:T(8,128)(2,1)S(1)}, u32[]{:S(2)}) copy-start(bf16[8,64,1,10,128]{4,1,0,3,2:T(8,128)(2,1)S(1)} %copy.50) | copy-start | bytes 3932164
  60.8 1.1 copy-start.7
  60.8 1.4 copy-start.8
  63.0 1.0 copy-start
  63.0 1.6 copy-start.2
  259.7 4.2 %copy-start.1 = (bf16[512,1,8,64]{3,0,2,1:T(8,128)(2,1)S(1)}, bf16[512,1,8,64]{3,0,2,1:T(8,128)(2,1)}, u32[]{:S(2)}) copy-start(bf16[512,1,8,64]{3,0,2,1:T(8,128)(2,1)} %copy-done) | copy-start | bytes 1572868
  259.7 4.2 %copy-start.4 = (pred[512,512]{0,1:T(8,128)(4,1)S(1)}, pred[512,512]{0,1:T(8,128)(4,1)}, u32[]{:S(2)}) copy-start(pred[512,512]{0,1:T(8,128)(4,1)} %iota_compare_fusion) | copy-start | bytes 786436
  267.4 1.8 copy-start.5
Sparse Core Ops, SparseCore 0:
  10.4 79.9 all-gather.2
  92.2 66.1 all-gather.4
where the time goes:
time: 321 us
  waiting for transfers between devices  128 us (40%)
  matrix products  75.1 us (23%)
  other arithmetic  45.3 us (14%)
  blocking collectives  38.6 us (12%)
  between operations  14.3 us (4%)
  starting transfers between devices  10.2 us (3%)
  local copies, waits for them, and re-layouts  8.6 us (3%)
    all_gather x1, waiting for transfers between devices, shards(): value_rows = lax.all_gather(prefix_values, 'outer', axis=0, tiled=True)  67.9 us
    dot_general x5, matrix products, absorb(): jnp.einsum('tkgd,nkd->tkgn', queries, key_rows, preferred_element_type=jn...  39.8 us
    all_to_all x1, blocking collectives, shards(): lax.all_to_all(outputs, 'inner', split_axis=0, concat_axis=1, tiled=True)  38.6 us
    reduce_sum x5, other arithmetic, absorb(): running_sum = running_sum * decay_factor + jnp.sum(weights, axis=-1)  35.7 us
    all_to_all x1, waiting for transfers between devices, shards(): lax.all_to_all(qkv, 'inner', split_axis=1, concat_axis=0, tiled=True)  35.3 us
    dot_general x5, matrix products, absorb(): jnp.einsum('tkgn,nkd->tkgd', weights.astype(jnp.bfloat16), value_rows, pr...  34.8 us
    all_gather x1, waiting for transfers between devices, shards(): key_rows = lax.all_gather(prefix_keys, 'outer', axis=0, tiled=True)  25.1 us
    all_to_all x1, starting transfers between devices, shards(): lax.all_to_all(qkv, 'inner', split_axis=1, concat_axis=0, tiled=True)  10.2 us
  transfers between devices with their start and end apart: 3, of which 3 were waited for; matrix products, arithmetic and copies ran while one was open for 2% of the time, Pallas kernels for 0%

commit v1 on v0

--- a/solution.py
+++ b/solution.py
@@ -70,7 +70,10 @@
     prefix_values = (value_codes.astype(jnp.float32) * value_scales[:, :, None]).astype(
         jnp.bfloat16
     )
-    exchanged = lax.all_to_all(qkv, "inner", split_axis=1, concat_axis=0, tiled=True)
+    size = lax.axis_size("inner")
+    blocks = jnp.stack(jnp.split(qkv, size, axis=1), axis=0)
+    blocks = lax.all_to_all(blocks, "inner", split_axis=0, concat_axis=0)
+    exchanged = jnp.concatenate(blocks, axis=0)
     stretch_rows = exchanged.shape[0]
     kv_local = exchanged.shape[1]
     local_pos = jnp.arange(stretch_rows, dtype=jnp.int32)

time: 321 us -> 320 us (level)
  waiting for transfers between devices: 128 us -> 122 us
  local copies, waits for them, and re-layouts: 8.6 us -> 13.2 us
    all_gather x1, waiting for transfers between devices: 25.1 us -> 18.5 us  [shards(): key_rows = lax.all_gather(prefix_keys, 'outer', axis=0, tiled=True)]
    unnamed x25 -> x27, local copies, waits for them, and re-layouts: 4.7 us -> 8.12 us
  transfers between devices with their start and end apart: 3 -> 3, of which waited for: 3 -> 3; matrix products, arithmetic and copies ran while one was open for 2% -> 4% of each run, Pallas kernels for 0% -> 0%
where the time goes in v1:
time: 320 us; the launch traced here: 319 us
  waiting for transfers between devices  122 us (38%)
  matrix products  74.6 us (23%)
  other arithmetic  45.3 us (14%)
  blocking collectives  38.6 us (12%)
  between operations  14.3 us (4%)
  local copies, waits for them, and re-layouts  13.2 us (4%)
  starting transfers between devices  10.4 us (3%)
    all_gather x1, waiting for transfers between devices, shards(): value_rows = lax.all_gather(prefix_values, 'outer', axis=0, tiled=True)  68.7 us
    dot_general x5, matrix products, absorb(): jnp.einsum('tkgd,nkd->tkgn', queries, key_rows, preferred_element_type=jn...  40.1 us
    all_to_all x1, blocking collectives, shards(): lax.all_to_all(outputs, 'inner', split_axis=0, concat_axis=1, tiled=True)  38.6 us
    reduce_sum x5, other arithmetic, absorb(): running_sum = running_sum * decay_factor + jnp.sum(weights, axis=-1)  35.7 us
    all_to_all x1, waiting for transfers between devices, shards(): blocks = lax.all_to_all(blocks, 'inner', split_axis=0, concat_axis=0)  35.1 us
    dot_general x5, matrix products, absorb(): jnp.einsum('tkgn,nkd->tkgd', weights.astype(jnp.bfloat16), value_rows, pr...  34 us
    all_gather x1, waiting for transfers between devices, shards(): key_rows = lax.all_gather(prefix_keys, 'outer', axis=0, tiled=True)  18.5 us
    all_to_all x1, starting transfers between devices, shards(): blocks = lax.all_to_all(blocks, 'inner', split_axis=0, concat_axis=0)  10.2 us
  transfers between devices with their start and end apart: 3, of which 3 were waited for; matrix products, arithmetic and copies ran while one was open for 4% of the time, Pallas kernels for 0%

profile of v1, /device:TPU:32, one launch (start us, length us, event | category | flops | bytes accessed | tf_op | source)
XLA Modules:
  0.0 319.0 jit_solution(16170967276454808180)
XLA Ops:
  10.3 2.2 fusion.78
  18.1 10.2 %all-to-all-start = ((bf16[8,64,1,10,128]{4,1,3,2,0:T(8,128)(2,1)}), bf16[8,64,1,10,128]{4,1,3,2,0:T(8,128)(2,1)S(1)}, u32[]{:S(2)}, u32[]{:S(2)}) async-start(bf16[8,64,1,10,128]{4,1,3,2,0:T(8,128)(2,1)} %fusion.50), calls=%async_computation | async-start | bytes 2621440 | tf_op jit(solution)/shard_map/all_to_all | solution.py:75
  30.1 1.8 multiply_cosine_fusion.1
  31.9 35.1 %all-to-all-done = bf16[8,64,1,10,128]{4,1,3,2,0:T(8,128)(2,1)S(1)} async-done(((bf16[8,64,1,10,128]{4,1,3,2,0:T(8,128)(2,1)}), bf16[8,64,1,10,128]{4,1,3,2,0:T(8,128)(2,1)S(1)}, u32[]{:S(2)}, u32[]{:S(2)}) %all-to-all-start) | async-done | bytes 1310752 | tf_op jit(solution)/shard_map/all_to_all | solution.py:75
  71.7 18.5 %all-gather.3.cloned.1.call-done = bf16[4096,1,128]{0,2,1:T(8,128)(2,1)} async-done(((bf16[128,1,128]{0,2,1:T(8,128)(2,1)}), bf16[4096,1,128]{0,2,1:T(8,128)(2,1)}) %all-gather.3.cloned.1.call-update) | async-done | bytes 1048592 | tf_op jit(solution)/shard_map/all_gather | solution.py:91
  90.2 68.7 %all-gather.5.cloned.1.call-done = bf16[4096,1,128]{0,2,1:T(8,128)(2,1)} async-done(((bf16[128,1,128]{0,2,1:T(8,128)(2,1)}), bf16[4096,1,128]{0,2,1:T(8,128)(2,1)}) %all-gather.5.cloned.1.call-update) | async-done | bytes 1048592 | tf_op jit(solution)/shard_map/all_gather | solution.py:92
  158.9 101.3 %while.18 = (s32[]{:T(128)}, f32[512,1,8]{0,2,1:T(8,128)S(1)}, f32[512,1,8]{0,2,1:T(8,128)S(1)}, f32[512,1,8,128]{0,3,2,1:T(8,128)S(1)}, bf16[4096,1,128]{0,2,1:...) while((s32[]{:T(128)}, f32[512,1,8]{0,2,1:T(8,128)S(1)}, ...), condition=%wide.region_3.0_spmd.clone, body=%wide.region_0.0_spmd.clone.sunk | while | flops 2182635520 | bytes 56361140 | solution.py:104
  158.9 9.1 %bitcast_reduce_fusion.2 = (f32[512,8]{0,1:T(8,128)S(1)}, f32[1024,512,8]{1,0,2:T(8,128)}) fusion(bf16[512,1,8,128]{3,0,2,1:T(8,128)(2,1)S(1)} %get-tuple-element.281, bf16[4096,1,128]{0,2,1:T(8,128)(2,1)} %get-tuple-element.280, s32[]{:T(128)S(6)} %select_n.27), kind=kOutput, calls=%fused_computation.1.clone.1 | convolution fusion | flops 1082126336 | bytes 18104324 | tf_op jit(solution)/shard_map/while/body/eval_jaxpr/tkgd,nkd->tkgn/dot_general | solution.py:47
  168.0 8.5 %fusion.86 = f32[512,8]{0,1:T(8,128)S(1)} fusion(f32[1024,512,8]{1,0,2:T(8,128)} %get-tuple-element.252, f32[512,8]{0,1:T(8,128)S(1)} %bitcast.193), kind=kLoop, calls=%fused_computation.4.clone.1 | loop fusion | flops 12578816 | bytes 16809984 | tf_op jit(solution)/shard_map/while/body/eval_jaxpr/reduce_sum | solution.py:55
  176.6 7.7 %bitcast_add_fusion.7 = f32[512,1,8,128]{0,3,2,1:T(8,128)S(1)} fusion(f32[512,1,8,128]{0,3,2,1:T(8,128)S(1)} %get-tuple-element.268, f32[1024,512,8]{1,0,2:T(8,128)} %get-tuple-element.252, f32[512,8]{0,1:T(8,128)S(1)} %bitcast.194, f32[512,8]{0,1:T(8,128)S(1)} %get-tuple-element.253, pred[]{:T(512)S(6)} %compare.3, ...), kind=kOutput, calls=%fused_computation.9.clone.1 | convolution fusion | flops 1087897600 | bytes 21266436 | tf_op jit(solution)/shard_map/while/body/eval_jaxpr/tkgn,nkd->tkgd/dot_general | solution.py:56
  184.3 9.1 %bitcast_reduce_fusion.2 = (f32[512,8]{0,1:T(8,128)S(1)}, f32[1024,512,8]{1,0,2:T(8,128)}) fusion(bf16[512,1,8,128]{3,0,2,1:T(8,128)(2,1)S(1)} %get-tuple-element.281, bf16[4096,1,128]{0,2,1:T(8,128)(2,1)} %get-tuple-element.280, s32[]{:T(128)S(6)} %select_n.27), kind=kOutput, calls=%fused_computation.1.clone.1 | convolution fusion | flops 1082126336 | bytes 18104324 | tf_op jit(solution)/shard_map/while/body/eval_jaxpr/tkgd,nkd->tkgn/dot_general | solution.py:47
  193.4 8.5 %fusion.86 = f32[512,8]{0,1:T(8,128)S(1)} fusion(f32[1024,512,8]{1,0,2:T(8,128)} %get-tuple-element.252, f32[512,8]{0,1:T(8,128)S(1)} %bitcast.193), kind=kLoop, calls=%fused_computation.4.clone.1 | loop fusion | flops 12578816 | bytes 16809984 | tf_op jit(solution)/shard_map/while/body/eval_jaxpr/reduce_sum | solution.py:55
  201.9 7.7 %bitcast_add_fusion.7 = f32[512,1,8,128]{0,3,2,1:T(8,128)S(1)} fusion(f32[512,1,8,128]{0,3,2,1:T(8,128)S(1)} %get-tuple-element.268, f32[1024,512,8]{1,0,2:T(8,128)} %get-tuple-element.252, f32[512,8]{0,1:T(8,128)S(1)} %bitcast.194, f32[512,8]{0,1:T(8,128)S(1)} %get-tuple-element.253, pred[]{:T(512)S(6)} %compare.3, ...), kind=kOutput, calls=%fused_computation.9.clone.1 | convolution fusion | flops 1087897600 | bytes 21266436 | tf_op jit(solution)/shard_map/while/body/eval_jaxpr/tkgn,nkd->tkgd/dot_general | solution.py:56
  209.6 9.1 %bitcast_reduce_fusion.2 = (f32[512,8]{0,1:T(8,128)S(1)}, f32[1024,512,8]{1,0,2:T(8,128)}) fusion(bf16[512,1,8,128]{3,0,2,1:T(8,128)(2,1)S(1)} %get-tuple-element.281, bf16[4096,1,128]{0,2,1:T(8,128)(2,1)} %get-tuple-element.280, s32[]{:T(128)S(6)} %select_n.27), kind=kOutput, calls=%fused_computation.1.clone.1 | convolution fusion | flops 1082126336 | bytes 18104324 | tf_op jit(solution)/shard_map/while/body/eval_jaxpr/tkgd,nkd->tkgn/dot_general | solution.py:47
  218.7 8.5 %fusion.86 = f32[512,8]{0,1:T(8,128)S(1)} fusion(f32[1024,512,8]{1,0,2:T(8,128)} %get-tuple-element.252, f32[512,8]{0,1:T(8,128)S(1)} %bitcast.193), kind=kLoop, calls=%fused_computation.4.clone.1 | loop fusion | flops 12578816 | bytes 16809984 | tf_op jit(solution)/shard_map/while/body/eval_jaxpr/reduce_sum | solution.py:55
  227.2 7.7 %bitcast_add_fusion.7 = f32[512,1,8,128]{0,3,2,1:T(8,128)S(1)} fusion(f32[512,1,8,128]{0,3,2,1:T(8,128)S(1)} %get-tuple-element.268, f32[1024,512,8]{1,0,2:T(8,128)} %get-tuple-element.252, f32[512,8]{0,1:T(8,128)S(1)} %bitcast.194, f32[512,8]{0,1:T(8,128)S(1)} %get-tuple-element.253, pred[]{:T(512)S(6)} %compare.3, ...), kind=kOutput, calls=%fused_computation.9.clone.1 | convolution fusion | flops 1087897600 | bytes 21266436 | tf_op jit(solution)/shard_map/while/body/eval_jaxpr/tkgn,nkd->tkgd/dot_general | solution.py:56
  234.9 9.1 %bitcast_reduce_fusion.2 = (f32[512,8]{0,1:T(8,128)S(1)}, f32[1024,512,8]{1,0,2:T(8,128)}) fusion(bf16[512,1,8,128]{3,0,2,1:T(8,128)(2,1)S(1)} %get-tuple-element.281, bf16[4096,1,128]{0,2,1:T(8,128)(2,1)} %get-tuple-element.280, s32[]{:T(128)S(6)} %select_n.27), kind=kOutput, calls=%fused_computation.1.clone.1 | convolution fusion | flops 1082126336 | bytes 18104324 | tf_op jit(solution)/shard_map/while/body/eval_jaxpr/tkgd,nkd->tkgn/dot_general | solution.py:47
  244.0 8.5 %fusion.86 = f32[512,8]{0,1:T(8,128)S(1)} fusion(f32[1024,512,8]{1,0,2:T(8,128)} %get-tuple-element.252, f32[512,8]{0,1:T(8,128)S(1)} %bitcast.193), kind=kLoop, calls=%fused_computation.4.clone.1 | loop fusion | flops 12578816 | bytes 16809984 | tf_op jit(solution)/shard_map/while/body/eval_jaxpr/reduce_sum | solution.py:55
  252.6 7.7 %bitcast_add_fusion.7 = f32[512,1,8,128]{0,3,2,1:T(8,128)S(1)} fusion(f32[512,1,8,128]{0,3,2,1:T(8,128)S(1)} %get-tuple-element.268, f32[1024,512,8]{1,0,2:T(8,128)} %get-tuple-element.252, f32[512,8]{0,1:T(8,128)S(1)} %bitcast.194, f32[512,8]{0,1:T(8,128)S(1)} %get-tuple-element.253, pred[]{:T(512)S(6)} %compare.3, ...), kind=kOutput, calls=%fused_computation.9.clone.1 | convolution fusion | flops 1087897600 | bytes 21266436 | tf_op jit(solution)/shard_map/while/body/eval_jaxpr/tkgn,nkd->tkgd/dot_general | solution.py:56
  260.2 2.4 fusion.62
  262.7 3.7 %fusion.22 = (f32[512,8]{0,1:T(8,128)S(1)}, f32[512,512,8]{1,0,2:T(8,128)S(1)}) fusion(pred[512,512]{0,1:T(8,128)(4,1)S(1)} %copy-done.4, bf16[512,8,64]{2,0,1:T(8,128)(2,1)} %bitcast.196, bf16[512,8,64]{2,0,1:T(8,128)(2,1)} %bitcast.195, bf16[512,64]{1,0:T(8,128)(2,1)S(1)} %get-tuple-element.194, bf16[512,64]{1,0:T(8,128)(2,1)S(1)} %get-tuple-element.193), kind=kOutput, calls=%fused_computation.29 | convolution fusion | flops 545517568 | bytes 9846784 | tf_op jit(solution)/shard_map/tkgd,nkd->tkgn/dot_general | solution.py:47
  266.4 1.7 fusion.20
  268.2 3.3 %fusion.28 = bf16[512,1,8,128]{0,3,2,1:T(8,128)(2,1)S(1)} fusion(f32[512,1,8,128]{0,3,2,1:T(8,128)S(1)} %get-tuple-element.131, f32[512,512,8]{1,0,2:T(8,128)S(1)} %get-tuple-element.202, f32[512,8]{0,1:T(8,128)S(1)} %fusion.73, pred[512,512]{0,1:T(8,128)(4,1)S(1)} %copy-done.4, f32[512,8]{0,1:T(8,128)S(1)} %get-tuple-element.198, ...), kind=kOutput, calls=%fused_computation.35 | convolution fusion | flops 547356672 | bytes 11976704 | tf_op jit(solution)/shard_map/tkgn,nkd->tkgd/dot_general | solution.py:56
  272.3 38.6 %all_to_all.23 = bf16[512,1,8,128]{3,2,1,0:T(8,128)(2,1)S(1)} all-to-all(bf16[512,1,8,128]{3,2,1,0:T(8,128)(2,1)S(1)} %copy.74), channel_id=1, replica_groups=mesh['outer'=32,'inner'=8] {'inner'}, dimensions={0} | all-to-all | bytes 2097152 | tf_op jit(solution)/shard_map/all_to_all | solution.py:112
  (66 shorter events, 17.1 us)
Async XLA Ops:
  6.5 3.8 %copy-start.2 = (bf16[64,8,10,128]{3,1,2,0:T(8,128)(2,1)S(1)}, bf16[64,8,10,128]{3,1,2,0:T(8,128)(2,1)}, u32[]{:S(2)}) copy-start(bf16[64,8,10,128]{3,1,2,0:T(8,128)(2,1)} %param.8) | copy-start | bytes 3932164
  6.5 83.6 %all-gather.3.cloned.1.call-start = ((), (), s32[]{:S(2)}) async-start(), calls=%async_computation.2 | async-start | bytes 1081344 | tf_op jit(solution)/shard_map/all_gather | solution.py:91
  16.0 12.5 %copy-start.7 = (bf16[128,1,128]{2,0,1:T(8,128)(2,1)S(1)}, bf16[128,1,128]{2,0,1:T(8,128)(2,1)}, u32[]{:S(2)}) copy-start(bf16[128,1,128]{2,0,1:T(8,128)(2,1)} %param.11) | copy-start | bytes 98308
  16.0 12.6 %copy-start.8 = (f32[128,1]{0,1:T(1,128)S(1)}, f32[128,1]{0,1:T(1,128)}, u32[]{:S(2)}) copy-start(f32[128,1]{0,1:T(1,128)} %param.12) | copy-start | bytes 1540
  18.1 48.9 %all-to-all-start = ((bf16[8,64,1,10,128]{4,1,3,2,0:T(8,128)(2,1)}), bf16[8,64,1,10,128]{4,1,3,2,0:T(8,128)(2,1)S(1)}, u32[]{:S(2)}, u32[]{:S(2)}) async-start(bf16[8,64,1,10,128]{4,1,3,2,0:T(8,128)(2,1)} %fusion.50), calls=%async_computation | async-start | bytes 2621440 | tf_op jit(solution)/shard_map/all_to_all | solution.py:75
  28.3 130.6 %all-gather.5.cloned.1.call-start = ((), (), s32[]{:S(2)}) async-start(), calls=%async_computation.3 | async-start | bytes 1081344 | tf_op jit(solution)/shard_map/all_gather | solution.py:92
  67.2 3.7 %copy-start.3 = (bf16[8,64,1,10,128]{4,1,0,3,2:T(8,128)(2,1)}, bf16[8,64,1,10,128]{4,1,0,3,2:T(8,128)(2,1)S(1)}, u32[]{:S(2)}) copy-start(bf16[8,64,1,10,128]{4,1,0,3,2:T(8,128)(2,1)S(1)} %copy.69) | copy-start | bytes 3932164
  67.2 1.1 copy-start.5
  67.2 1.4 copy-start.6
  69.4 1.0 copy-start
  69.4 1.5 copy-start.1
  158.9 103.8 %copy-start.4 = (pred[512,512]{0,1:T(8,128)(4,1)S(1)}, pred[512,512]{0,1:T(8,128)(4,1)}, u32[]{:S(2)}) copy-start(pred[512,512]{0,1:T(8,128)(4,1)} %iota_compare_fusion) | copy-start | bytes 786436
Sparse Core Ops, SparseCore 0:
  10.4 79.6 all-gather.2
  91.9 66.9 all-gather.4
